TPU v7x, 256 devices: a whole 4x4x8 slice. The times are simulated.
256 devices in a mesh: lat: 64 (over x, z_lo, y, core), chan: 4 (over z_hi).
Axes of the slice: x: 4, y: 4, z: 8 (z_hi: 4, z_lo: 2; z = z_hi * 2 + z_lo), core: 2. Of those that a mesh axis runs over, the one named last changes fastest.
Arguments:
- grid_field: float32 [128, 1440, 256], P('lat', 'chan'), may hold values from -6 to 6
- filters: float32 [128, 4, 3, 5], P('lat'), may hold values from -1.5 to 1.5
- disco_weight: float32 [4, 256], replicated, may hold values from -3 to 3
- band_start: int32 [128], P('lat'), may hold values from -2 to 0
- band_reach: int32 [128], P('lat'), may hold values from 1 to 3
- spec_weight: float32 [256, 256], replicated, may hold values from -0.375 to 0.375
- degree_gain: float32 [360, 256], replicated, may hold values from 0.5 to 2
- cotangent: float32 [128, 1440, 256], P('lat', 'chan'), may hold values from -6 to 6
Outputs:
- output: float32 [128, 1440, 256], P('lat', 'chan')
- grad_input: float32 [128, 1440, 256], P('lat', 'chan')
- grad_weight: float32 [256, 256], replicated
Inputs may be any that keep to these rules, and one draw needn't show every extreme that they name: The block of latitude i covers rows i + band_start[i] to i + band_start[i] + 2. Rows of a block at or past band_reach[i] are padding.
All inputs are finite; a program needn't handle non-finite values.
Results may differ from a plain program's by a relative error of at most 0.0003.
Values sent between devices are 32-bit elements; how exact they have to be, the bound alone decides.
A program may use at most 64 MiB of HBM per device.

v0:
```python
import functools
import math

import jax
import jax.numpy as jnp
import ml_dtypes
import numpy as np
from jax import lax
from jax.experimental import pallas as pl
from jax.experimental.pallas import tpu as pltpu
from jax.sharding import PartitionSpec as P

L = 360
M = 256
WIN = 3
HMAX = 2
KLON = 5
POLAR = 720
SPAN = 2 * HMAX + 1
EDGE = 8
TAPS = 8
CLASSES = (0, 2, 1, 3)
STEPS = 4

highest = lax.Precision.HIGHEST
upper_bound = 2.0**32
lower_factor = 2.0 ** (-32)
log_step = 32.0 * math.log(2.0)
bf16 = jnp.bfloat16
f32 = jnp.float32


def padded_size(n):
    return -(-n // 128) * 128


def chunk_rows(n):
    return 72 if n % 72 == 0 else n


def grid_tables(lat_total):
    first_row = (POLAR - lat_total) // 2
    colatitude = math.pi * (jnp.arange(lat_total, dtype=jnp.float32) + float(first_row)) / POLAR
    quad_weight = 2.0 * math.pi * math.pi / POLAR * jnp.sin(colatitude)
    return (colatitude, quad_weight)


def log_norms(order_count):
    order_index = jnp.arange(order_count, dtype=jnp.float32)
    log_terms = jnp.where(
        order_index > 0.0,
        jnp.log((2.0 * order_index + 1.0) / jnp.maximum(2.0 * order_index, 1.0)),
        0.0,
    )
    return -0.5 * math.log(4.0 * math.pi) + 0.5 * jnp.cumsum(log_terms)


def filter_coeff(filters, disco_weight, band_start, band_reach, first_row, lat_total):
    count = filters.shape[0]
    rows = jnp.arange(WIN, dtype=jnp.int32)
    offsets = jnp.arange(SPAN, dtype=jnp.int32) - HMAX
    live = rows[None, :] < band_reach[:, None]
    place = (band_start[:, None] + rows[None, :])[:, :, None] == offsets[None, None, :]
    target = first_row + jnp.arange(count, dtype=jnp.int32)[:, None] + offsets[None, :]
    inside = (target >= 0) & (target < lat_total)
    chosen = jnp.where(live[:, :, None] & place & inside[:, None, :], 1.0, 0.0)
    placed = jnp.einsum("ikrt,iro->ikot", filters, chosen, precision=highest)
    placed = jnp.pad(placed, ((0, 0), (0, 0), (0, 0), (0, TAPS - KLON)))
    return jnp.einsum("ikot,kc->iotc", placed, disco_weight, precision=highest)


def owned_orders(lat_index, per_device, devices):
    per_class = devices // 4
    kind = lat_index // per_class
    kind_order = jnp.where(kind == 1, 2, jnp.where(kind == 2, 1, kind))
    local = (lat_index % per_class) * per_device + jnp.arange(per_device, dtype=jnp.int32)
    return kind_order + 4 * local


def halves(array):
    high = array.astype(ml_dtypes.bfloat16)
    low = (array - high.astype(np.float64)).astype(ml_dtypes.bfloat16)
    return np.stack([high, low], axis=0)


def wave_tables(quarter, lon_total):
    lon = np.arange(quarter)
    plain, first, second = ([], [], [])
    for kind in CLASSES:
        order = kind + 4 * np.arange(M // 4)
        angle = (order[:, None] * lon[None, :] % lon_total) * (2.0 * math.pi / lon_total)
        cosine, sine = (np.cos(angle), np.sin(angle))
        direct = np.stack([cosine, -sine], axis=1).reshape(M // 2, quarter)
        if kind % 2 == 0:
            plain.append(direct)
        else:
            sign = 1.0 if kind == 1 else -1.0
            first.append(direct)
            second.append(np.stack([-sign * sine, -sign * cosine], axis=1).reshape(M // 2, quarter))
    table = np.concatenate(plain + first + second, axis=0)
    table = np.pad(table, ((0, 0), (0, padded_size(quarter) - quarter)))
    return (halves(table), halves(np.ascontiguousarray(table.T)))


def split(x):
    high = x.astype(bf16)
    low = (x - high.astype(f32)).astype(bf16)
    return (high, low)


def side_by_side(x):
    high, low = split(x)
    return jnp.concatenate([high, low], axis=1)


def dot(a, b):
    return jnp.dot(a, b, preferred_element_type=f32)


def folded(y):
    half = y.shape[1] // 2
    return y[:, :half] + y[:, half:]


def swap_halves(a, b):
    low = lax.broadcasted_iota(jnp.int32, a.shape, 1) < 64
    first = jnp.where(low, a, pltpu.roll(b, 64, 1))
    second = jnp.where(low, pltpu.roll(a, 64, 1), b)
    return (first, second)


def layer_kernel(
    f_ref, cot_ref, w_ref, coef_ref, gain_ref, small_ref, qw_ref, tf_ref, ti_ref,
    out_ref, gin_ref, gw_ref,
    z1, g1, y1, h1, z2, g2, y2, h2,
    s1, r1, o1, c1, s2, r2, o2, c2,
    wsend, wrecv, wpart, wall, wmine,
    fext, eext, cext, local, gpad, ft_ref, leg_ref, l2_ref, lt_ref,
    chan_send, chan_recv, lat_send, lat_recv, own_sem, halo_send, halo_recv, coef_send, coef_recv,
):
    devices = lax.axis_size("lat")
    me = lax.axis_index("lat")
    mine = lax.axis_index("chan")
    rows, quarter, chans = f_ref.shape
    qp = g1.shape[1]
    lp = l2_ref.shape[1]
    step = chunk_rows(quarter)
    up = lax.rem(me + 1, devices)
    down = lax.rem(me + devices - 1, devices)
    right = lax.rem(mine + 1, 4)
    left = lax.rem(mine + 3, 4)

    barrier = pltpu.get_barrier_semaphore()

    def greet(k, carry):
        pl.semaphore_signal(barrier, inc=1, device_id={"lat": lax.rem(me + k, devices)})
        return carry

    lax.fori_loop(1, devices, greet, 0)
    for k in range(1, 4):
        pl.semaphore_signal(barrier, inc=1, device_id={"chan": lax.rem(mine + k, 4)})
    for a in (up, down):
        for b in (right, left):
            pl.semaphore_signal(barrier, inc=1, device_id={"lat": a, "chan": b})

    def pack(buffer, i, h, pair):
        buffer[2 * h, pl.ds(i, pair[0].shape[0]), :] = pair[0]
        buffer[2 * h + 1, pl.ds(i, pair[0].shape[0]), :] = pair[1]

    w_high, w_low = split(w_ref[...])
    mixed = []
    for i in range(rows):
        high, low = split(f_ref[i])
        mixed.append(dot(high, w_high) + (dot(low, w_high) + dot(high, w_low)))
    for h in range(2):
        lanes = slice(128 * h, 128 * h + 128)
        pack(z1, 0, h, swap_halves(mixed[0][:, lanes], mixed[1][:, lanes]))

    pl.semaphore_wait(barrier, devices - 1 + 3 + 4)

    def chan_start(stage, source, target):
        copies = []
        for k in (2, 1, 3):
            peer = lax.rem(mine + k, 4)
            copy = pltpu.make_async_remote_copy(
                src_ref=source.at[peer, pl.ds(0, quarter)],
                dst_ref=target.at[mine, pl.ds(0, quarter)],
                send_sem=chan_send.at[stage, k],
                recv_sem=chan_recv.at[stage, k],
                device_id={"chan": peer},
            )
            copy.start()
            copies.append(copy)
        own = pltpu.make_async_copy(
            source.at[mine, pl.ds(0, quarter)], target.at[mine, pl.ds(0, quarter)], own_sem.at[stage]
        )
        own.start()
        return (copies, own)

    def chan_wait(handle):
        copies, own = handle
        own.wait()
        for copy in copies:
            copy.wait_recv()

    def lat_start(stage, source, target, size, spread=False):
        def send(k, carry):
            peer = lax.rem(me + k, devices)
            first = 0 if spread else pl.multiple_of(peer * size, 8)
            pltpu.make_async_remote_copy(
                src_ref=source.at[pl.ds(first, size)],
                dst_ref=target.at[pl.ds(pl.multiple_of(me * size, 8), size)],
                send_sem=lat_send.at[stage],
                recv_sem=lat_recv.at[stage],
                device_id={"lat": peer},
            ).start()
            return carry

        lax.fori_loop(1, devices, send, 0)
        first = 0 if spread else pl.multiple_of(me * size, 8)
        pltpu.make_async_copy(
            source.at[pl.ds(first, size)],
            target.at[pl.ds(pl.multiple_of(me * size, 8), size)],
            lat_recv.at[stage],
        ).start()

    def lat_wait(stage, target):
        pltpu.make_async_copy(target, target, lat_recv.at[stage]).wait()

    def lat_drain(stage, target, size):
        sent = target.at[pl.ds(0, size * (devices - 1))]
        pltpu.make_async_copy(sent, sent, lat_send.at[stage]).wait()

    def halo_start(stage, ext, field):
        whole = pl.ds(EDGE, quarter)
        low, high = (pl.ds(0, EDGE), pl.ds(EDGE + quarter, EDGE))
        above, here, below = (pl.ds(0, 2), pl.ds(2, 2), pl.ds(4, 2))
        last = field(pl.ds(quarter - EDGE, EDGE))
        first = field(pl.ds(0, EDGE))
        everything = field(pl.ds(0, quarter))
        moves = [
            (last, here, low, me, right), (first, here, high, me, left),
            (last, above, low, up, right), (first, above, high, up, left),
            (last, below, low, down, right), (first, below, high, down, left),
            (everything, above, whole, up, mine), (everything, below, whole, down, mine),
        ]
        copies = []
        for index, (source, row, col, a, b) in enumerate(moves):
            copy = pltpu.make_async_remote_copy(
                src_ref=source,
                dst_ref=ext.at[row, col],
                send_sem=halo_send.at[stage, index],
                recv_sem=halo_recv.at[stage, index],
                device_id={"lat": a, "chan": b},
            )
            copy.start()
            copies.append(copy)
        return copies

    first_exchange = chan_start(0, z1, g1)
    own_field = pltpu.make_async_copy(f_ref, fext.at[pl.ds(2, 2), pl.ds(EDGE, quarter)], own_sem.at[4])
    own_field.start()
    own_coef = pltpu.make_async_copy(coef_ref, cext.at[pl.ds(2, 2)], own_sem.at[5])
    own_coef.start()
    coef_copies = []
    for index, (peer, row) in enumerate(((up, 0), (down, 4))):
        copy = pltpu.make_async_remote_copy(
            src_ref=coef_ref,
            dst_ref=cext.at[pl.ds(row, 2)],
            send_sem=coef_send.at[index],
            recv_sem=coef_recv.at[index],
            device_id={"lat": peer},
        )
        copy.start()
        coef_copies.append(copy)
    field_halo = halo_start(0, fext, lambda cols: f_ref.at[:, cols])

    order, start, log_start, cosine = (small_ref[0], small_ref[1], small_ref[2], small_ref[3])
    order_square = order * order
    zeros = jnp.zeros_like(order)

    def recur(index, carry):
        previous, second, log_scale = carry
        scale = jnp.exp(log_scale)
        for offset in range(STEPS):
            degree = (index * STEPS + offset).astype(f32)
            square = degree * degree
            lower = degree - 1.0
            lower_square = lower * lower
            factor = jnp.where(
                order < degree,
                jnp.sqrt(jnp.maximum(4.0 * square - 1.0, 0.0) / jnp.maximum(square - order_square, 1.0)),
                0.0,
            )
            back = jnp.sqrt(jnp.maximum(lower_square - order_square, 0.0) / (4.0 * lower_square - 1.0))
            rest = jnp.where(order == degree, start, 0.0) - (factor * back) * second
            current = (factor * cosine) * previous + rest
            leg_ref[pl.ds(pl.multiple_of((index * STEPS + offset) * 8, 8), 8), :] = current * scale
            second = previous
            previous = current
        too_large = jnp.maximum(jnp.abs(previous), jnp.abs(second)) > upper_bound
        previous = jnp.where(too_large, previous * lower_factor, previous)
        second = jnp.where(too_large, second * lower_factor, second)
        log_scale = jnp.where(too_large, log_scale + log_step, log_scale)
        return (previous, second, log_scale)

    lax.fori_loop(0, L // STEPS, recur, (zeros, zeros, log_start))
    lats = 2 * devices
    if lp > L:
        leg_ref[pl.ds(8 * L, 8 * (lp - L)), :] = jnp.zeros((8 * (lp - L), leg_ref.shape[1]), f32)
    for m in range(4):
        table = leg_ref[pl.ds(m, lp, stride=8), :]
        l2_ref[m] = side_by_side(table)
        high, low = split(table.T)
        lt_ref[m, 0] = high
        lt_ref[m, 1] = low
    for i in range(rows):
        field = f_ref[i]
        if qp > quarter:
            field = jnp.concatenate([field, jnp.zeros((qp - quarter, chans), f32)], axis=0)
            gpad[i, pl.ds(quarter, qp - quarter), :] = jnp.zeros((qp - quarter, chans), f32)
        high, low = split(field.T)
        ft_ref[i, 0] = high
        ft_ref[i, 1] = low

    def waves_forward(grid, spec):
        def block(q):
            value = grid[q, pl.ds(0, quarter), :]
            if qp > quarter:
                value = jnp.concatenate([value, jnp.zeros((qp - quarter, 128), f32)], axis=0)
            return value

        g_0, g_1, g_2, g_3 = (block(0), block(1), block(2), block(3))
        even, odd = (g_0 + g_2, g_1 + g_3)
        half = 2 * devices

        def apply(first, count, data):
            band = pl.ds(first, count)
            return dot(tf_ref[0, band, :], data) + dot(tf_ref[1, band, :], data)

        spec[pl.ds(0, half), :] = folded(apply(0, half, side_by_side(even + odd)))
        spec[pl.ds(half, half), :] = folded(apply(half, half, side_by_side(even - odd)))
        u, v = (side_by_side(g_0 - g_2), side_by_side(g_1 - g_3))
        spec[pl.ds(2 * half, 2 * half), :] = folded(
            apply(2 * half, 2 * half, u) + apply(4 * half, 2 * half, v)
        )

    def waves_inverse(spec, grid):
        half = 2 * devices

        def apply(first, count, data):
            return folded(
                dot(ti_ref[0, :, first : first + count], data)
                + dot(ti_ref[1, :, first : first + count], data)
            )

        plain = apply(0, half, side_by_side(spec[pl.ds(0, half), :]))
        other = apply(half, half, side_by_side(spec[pl.ds(half, half), :]))
        cross = side_by_side(spec[pl.ds(2 * half, 2 * half), :])
        u = apply(2 * half, 2 * half, cross)
        v = apply(4 * half, 2 * half, cross)
        even, odd = (plain + other, plain - other)
        for q, value in enumerate((even + u, odd + v, even - u, odd - v)):
            grid[q] = value

    def legendre_pair(spec, result, weigh_first):
        for m in range(4):
            r_0 = spec[pl.ds(2 * m, devices, stride=8), :]
            r_1 = spec[pl.ds(2 * m + 1, devices, stride=8), :]
            x = jnp.concatenate(swap_halves(r_0, r_1), axis=0)
            if weigh_first:
                x = x * qw_ref[m]
            data = side_by_side(x)
            data = jnp.concatenate([data, data], axis=0)
            degree = folded(dot(l2_ref[m], data)) * gain_ref[...]
            data = side_by_side(degree)
            s = folded(dot(lt_ref[m, 0], data) + dot(lt_ref[m, 1], data))
            if not weigh_first:
                s = s * qw_ref[m]
            t_0, t_1 = swap_halves(s[:devices], s[devices:])
            result[pl.ds(2 * m, devices, stride=8), :] = t_0
            result[pl.ds(2 * m + 1, devices, stride=8), :] = t_1

    def spectral_path(exchange, stage, grid, spec, arrived, back, returned, result, final, weigh_first):
        chan_wait(exchange)
        waves_forward(grid, spec)
        lat_start(stage, spec, arrived, 8)
        lat_wait(stage, arrived)
        legendre_pair(arrived, back, weigh_first)
        lat_start(stage + 1, back, returned, 8)
        lat_wait(stage + 1, returned)
        waves_inverse(returned, result)
        return chan_start(stage + 1, result, final)

    def local_filter(ext, weights, adjoint, n, h):
        lanes = pl.ds(128 * h, 128)
        totals = [None] * rows
        for plane in range(rows + 2 * HMAX):
            value = ext[plane, pl.ds(n, step + 2 * EDGE), lanes]
            for t in range(KLON):
                shift = EDGE + (2 - t if adjoint else t - 2)
                moved = value[shift : shift + step]
                for i in range(rows):
                    o = i + 2 * HMAX - plane if adjoint else plane - i
                    if 0 <= o < SPAN:
                        source = plane if adjoint else i
                        term = weights[source, o, pl.ds(t, 1), lanes] * moved
                        totals[i] = term if totals[i] is None else totals[i] + term
        return totals

    second_exchange = spectral_path(first_exchange, 0, g1, s1, r1, o1, c1, y1, h1, True)

    own_field.wait()
    for copy in field_halo:
        copy.wait_recv()

    def forward_local(index, carry):
        n = pl.multiple_of(index * step, 8)
        for h in range(2):
            totals = local_filter(fext, coef_ref, False, n, h)
            for i in range(rows):
                local[i, pl.ds(n, step), pl.ds(128 * h, 128)] = totals[i]
        return carry

    lax.fori_loop(0, quarter // step, forward_local, 0)

    chan_wait(second_exchange)

    def pointwise(index, carry):
        n = pl.multiple_of(index * step, 8)
        band = pl.ds(n, step)
        for h in range(2):
            lanes = pl.ds(128 * h, 128)
            spectral = swap_halves(h1[2 * h, band, :], h1[2 * h + 1, band, :])
            errors = []
            for i in range(rows):
                hidden = local[i, band, lanes] + spectral[i]
                gate = 1.0 / (1.0 + jnp.exp(-hidden))
                out_ref[i, band, lanes] = f_ref[i, band, lanes] + hidden * gate
                error = cot_ref[i, band, lanes] * (gate * (1.0 + hidden * (1.0 - gate)))
                eext[2 + i, pl.ds(pl.multiple_of(n + EDGE, 8), step), lanes] = error
                errors.append(error)
            pack(z2, n, h, swap_halves(errors[0], errors[1]))
        return carry

    lax.fori_loop(0, quarter // step, pointwise, 0)

    third_exchange = chan_start(2, z2, g2)

    def error_part(cols):
        return eext.at[pl.ds(2, 2), pl.ds(cols.start + EDGE, cols.size)]

    error_halo = halo_start(1, eext, error_part)
    last_exchange = spectral_path(third_exchange, 2, g2, s2, r2, o2, c2, y2, h2, False)

    own_coef.wait()
    for copy in coef_copies + error_halo:
        copy.wait_recv()

    def backward_local(index, carry):
        n = pl.multiple_of(index * step, 8)
        for h in range(2):
            totals = local_filter(eext, cext, True, n, h)
            for i in range(rows):
                local[i, pl.ds(n, step), pl.ds(128 * h, 128)] = totals[i]
        return carry

    lax.fori_loop(0, quarter // step, backward_local, 0)

    chan_wait(last_exchange)
    for h in range(2):
        band = pl.ds(0, quarter)
        pair = swap_halves(h2[2 * h, band, :], h2[2 * h + 1, band, :])
        for i in range(rows):
            gpad[i, band, pl.ds(128 * h, 128)] = pair[i]

    weight = jnp.zeros((chans, chans), f32)
    for i in range(rows):
        high, low = split(gpad[i])
        weight = weight + dot(ft_ref[i, 0], high) + (dot(ft_ref[i, 1], high) + dot(ft_ref[i, 0], low))
    wsend[pl.ds(0, chans), :] = weight[:, :128]
    wsend[pl.ds(chans, chans), :] = weight[:, 128:]
    piece = 2 * chans // devices
    lat_start(4, wsend, wrecv, piece)

    transposed = (((1,), (1,)), ((), ()))

    def dot_t(a, b):
        return lax.dot_general(a, b, transposed, preferred_element_type=f32)

    for i in range(rows):
        high, low = split(gpad[i, pl.ds(0, quarter), :])
        grad = dot_t(high, w_high) + (dot_t(low, w_high) + dot_t(high, w_low))
        gin_ref[i] = cot_ref[i] + local[i] + grad

    lat_wait(4, wrecv)
    total = wrecv[pl.ds(0, piece), :]
    for k in range(1, devices):
        total = total + wrecv[pl.ds(k * piece, piece), :]
    wmine[...] = total
    copies = []
    for k in range(1, 4):
        peer = lax.rem(mine + k, 4)
        copy = pltpu.make_async_remote_copy(
            src_ref=wmine,
            dst_ref=wpart.at[mine],
            send_sem=chan_send.at[4, k],
            recv_sem=chan_recv.at[4, k],
            device_id={"chan": peer},
        )
        copy.start()
        copies.append(copy)
    own = pltpu.make_async_copy(wmine, wpart.at[mine], own_sem.at[6])
    own.start()
    own.wait()
    for copy in copies:
        copy.wait_recv()
        copy.wait_send()
    wsum = wpart[0] + wpart[1] + wpart[2] + wpart[3]
    wmine[...] = wsum
    lat_start(5, wmine, wall, piece, spread=True)
    lat_wait(5, wall)
    gw_ref[:, pl.ds(0, 128)] = wall[pl.ds(0, chans), :]
    gw_ref[:, pl.ds(128, 128)] = wall[pl.ds(chans, chans), :]

    for handle in (first_exchange, second_exchange, third_exchange, last_exchange):
        for copy in handle[0]:
            copy.wait_send()
    for copy in field_halo + error_halo + coef_copies:
        copy.wait_send()
    for stage, buffer in enumerate((s1, o1, s2, o2)):
        lat_drain(stage, buffer, 8)
    lat_drain(4, wsend, piece)
    lat_drain(5, wall, piece)


def body(
    grid_field, filters, disco_weight, band_start, band_reach, spec_weight, degree_gain, cotangent
):
    rows, quarter, chans = grid_field.shape
    lat_devices = lax.axis_size("lat")
    chan_devices = lax.axis_size("chan")
    lat_total = rows * lat_devices
    lon_total = quarter * chan_devices
    part = chans // chan_devices
    per_device = M // lat_devices
    qp, lp = (padded_size(quarter), padded_size(L))
    me = lax.axis_index("lat")

    colatitude, quad_weight = grid_tables(lat_total)
    colatitude = colatitude.reshape(lat_devices, rows).T.reshape(-1)
    quad_weight = quad_weight.reshape(lat_devices, rows).T.reshape(-1)
    orders = owned_orders(me, per_device, lat_devices)
    one_hot = (orders[:, None] == jnp.arange(M, dtype=jnp.int32)[None, :]).astype(f32)
    log_norm = jnp.sum(one_hot * log_norms(M)[None, :], axis=1)
    order_f = orders.astype(f32)[:, None]
    shape = (per_device, lat_total)
    small = jnp.stack(
        [
            jnp.broadcast_to(order_f, shape),
            jnp.broadcast_to(jnp.exp(log_norm)[:, None], shape),
            order_f * jnp.log(jnp.sin(colatitude))[None, :],
            jnp.broadcast_to(jnp.cos(colatitude)[None, :], shape),
        ],
        axis=0,
    )
    small = jnp.concatenate([small, small], axis=1)
    order_weight = jnp.where(orders == 0, 1.0, 2.0).astype(f32) / lon_total
    qw = jnp.broadcast_to(
        order_weight[:, None, None] * quad_weight[None, :, None], (per_device, lat_total, 128)
    )
    gain = lax.dynamic_slice_in_dim(degree_gain, lax.axis_index("chan") * part, part, axis=1)
    gain = jnp.pad(jnp.concatenate([gain, gain], axis=1), ((0, lp - L), (0, 0)))
    coefficient = filter_coeff(
        filters, disco_weight, band_start, band_reach, me * rows, lat_total
    )
    tables, inverse = wave_tables(quarter, lon_total)

    block = pltpu.VMEM((chan_devices, qp, 128), f32)
    line = pltpu.VMEM((8 * lat_devices, 128), f32)
    weights = pltpu.VMEM((2 * chans, 128), f32)
    piece = 2 * chans // lat_devices
    extended = pltpu.VMEM((rows + 2 * HMAX, quarter + 2 * EDGE, chans), f32)
    dma = pltpu.SemaphoreType.DMA
    scratch = (
        [block] * 8
        + [line] * 8
        + [
            weights,
            weights,
            pltpu.VMEM((4, piece, 128), f32),
            weights,
            pltpu.VMEM((piece, 128), f32),
            extended,
            extended,
            pltpu.VMEM((rows + 2 * HMAX, SPAN, TAPS, chans), f32),
            pltpu.VMEM((rows, quarter, chans), f32),
            pltpu.VMEM((rows, qp, chans), f32),
            pltpu.VMEM((rows, 2, chans, qp), bf16),
            pltpu.VMEM((8 * lp, lat_total), f32),
            pltpu.VMEM((4, lp, 2 * lat_total), bf16),
            pltpu.VMEM((4, 2, lat_total, lp), bf16),
            dma((5, 4)),
            dma((5, 4)),
            dma((6,)),
            dma((6,)),
            dma((7,)),
            dma((2, 8)),
            dma((2, 8)),
            dma((2,)),
            dma((2,)),
        ]
    )
    vmem = pl.BlockSpec(memory_space=pltpu.VMEM)
    return pl.pallas_call(
        layer_kernel,
        out_shape=(
            jax.ShapeDtypeStruct(grid_field.shape, f32),
            jax.ShapeDtypeStruct(grid_field.shape, f32),
            jax.ShapeDtypeStruct((chans, chans), f32),
        ),
        in_specs=[vmem] * 9,
        out_specs=(vmem, vmem, vmem),
        scratch_shapes=scratch,
        compiler_params=pltpu.CompilerParams(
            collective_id=0, has_side_effects=True, vmem_limit_bytes=60 * 1024 * 1024
        ),
        name="layer",
    )(
        grid_field,
        cotangent,
        spec_weight,
        coefficient,
        gain,
        small,
        qw,
        jnp.asarray(tables),
        jnp.asarray(inverse),
    )


def solution(mesh):
    in_specs = (
        P("lat", "chan", None),
        P("lat", None, None, None),
        P(),
        P("lat"),
        P("lat"),
        P(),
        P(),
        P("lat", "chan", None),
    )
    out_specs = (P("lat", "chan", None), P("lat", "chan", None), P())
    return jax.shard_map(body, mesh=mesh, in_specs=in_specs, out_specs=out_specs, check_vma=False)
```

profile of v0, /device:TPU:1, one launch (start us, length us, event | category | flops | bytes accessed | tf_op | source)
XLA Modules:
  0.0 168.0 jit_solution(6860110877852716052)
XLA Ops:
  0.6 0.0 copy-start
  0.7 0.1 compare_and_fusion
  0.8 0.7 iota_compare_fusion.2
  1.5 0.7 iota_add_fusion
  2.3 0.1 fusion.18
  2.3 0.1 reshape.244
  2.4 0.1 broadcast_multiply_fusion.2
  2.4 0.1 reshape.246
  2.5 0.1 broadcast_multiply_fusion
  2.7 0.1 reshape.243
  2.8 0.3 reduce-window.9
  3.1 0.1 slice.7
  3.2 0.1 slice_reduce_fusion
  3.3 0.1 add_bitcast_fusion
  3.4 0.2 select_reduce_fusion
  3.6 0.1 stack_broadcast_in_dim.7
  3.7 0.1 broadcast_multiply_fusion.1
  3.7 0.1 stack_broadcast_in_dim.6
  3.8 0.6 maximum_maximum_fusion.small_ref
  4.4 1.0 convolution_bitcast_fusion
  5.4 1.6 fusion.coef_ref
  7.0 0.0 copy-done
  7.0 0.1 constant_dynamic-slice_fusion
  7.2 0.8 select_maximum_fusion.gain_ref
  8.0 0.8 broadcast_in_dim.22.qw_ref
  8.8 155.5 %layer.1 = (f32[2,360,256]{2,1,0:T(8,128)}, f32[2,360,256]{2,1,0:T(8,128)}, f32[256,256]{1,0:T(8,128)}) custom-call(f32[2,360,256]{2,1,0:T(8,128)} %f_ref.1, f32[2,360,256]{2,1,0:T(8,128)} %cot_ref.1, f32[256,256]{1,0:T(8,128)} %w_ref.1, f32[2,5,8,256]{3,2,1,0:T(8,128)} %fusion.coef_ref, f32[384,128]{1,0:T(8,128)} %select_maximum_fusion.gain_ref, ...), custom_call_target="tpu_custom_call" | custom-call | tf_op jit(solution)/shard_map/layer/pallas_call | solution.py:615
  164.3 0.0 copy-start.1
  164.3 0.0 copy-start.2
  164.3 2.1 %copy.23 = f32[2,360,256]{2,1,0:T(8,128)} copy(f32[2,360,256]{2,1,0:T(8,128)} %get-tuple-element.8) | data formatting | bytes 1474560
  166.4 0.0 copy-done.1
  166.4 0.9 copy.24
  167.3 0.0 copy-done.2
  167.3 0.7 copy.25
  (10 shorter events, 0.1 us)
Async XLA Ops:
  0.6 6.4 %copy-start = (f32[360,256]{1,0:T(8,128)S(1)}, f32[360,256]{1,0:T(8,128)}, u32[]{:S(2)}) copy-start(f32[360,256]{1,0:T(8,128)} %param.16) | copy-start | bytes 1105924
  164.3 2.1 %copy-start.1 = (f32[2,360,256]{2,1,0:T(8,128)S(1)}, f32[2,360,256]{2,1,0:T(8,128)}, u32[]{:S(2)}) copy-start(f32[2,360,256]{2,1,0:T(8,128)} %get-tuple-element.9) | copy-start | bytes 2211844
  164.3 3.0 %copy-start.2 = (f32[256,256]{1,0:T(8,128)S(1)}, f32[256,256]{1,0:T(8,128)}, u32[]{:S(2)}) copy-start(f32[256,256]{1,0:T(8,128)} %get-tuple-element.10) | copy-start | bytes 786436
where the time goes:
time: 168 us
  Pallas kernels  155 us (92%)
  local copies, waits for them, and re-layouts  5.23 us (3%)
  other arithmetic  3.89 us (2%)
  matrix products  2.6 us (2%)
    pallas_call x1, Pallas kernels, body(): pl.pallas_call(layer_kernel, out_shape=(jax.ShapeDtypeStruct(grid_field.s...  155 us
    unnamed x10, local copies, waits for them, and re-layouts  3.7 us

commit v1 on v0

--- a/solution.py
+++ b/solution.py
@@ -1,4 +1,3 @@
-import functools
 import math
 
 import jax
@@ -38,21 +37,22 @@
     return 72 if n % 72 == 0 else n
 
 
-def grid_tables(lat_total):
+def geometry(lat_devices, rows, per_device):
+    lat_total = lat_devices * rows
     first_row = (POLAR - lat_total) // 2
-    colatitude = math.pi * (jnp.arange(lat_total, dtype=jnp.float32) + float(first_row)) / POLAR
-    quad_weight = 2.0 * math.pi * math.pi / POLAR * jnp.sin(colatitude)
-    return (colatitude, quad_weight)
-
-
-def log_norms(order_count):
-    order_index = jnp.arange(order_count, dtype=jnp.float32)
-    log_terms = jnp.where(
-        order_index > 0.0,
-        jnp.log((2.0 * order_index + 1.0) / jnp.maximum(2.0 * order_index, 1.0)),
-        0.0,
-    )
-    return -0.5 * math.log(4.0 * math.pi) + 0.5 * jnp.cumsum(log_terms)
+    colatitude = math.pi * (np.arange(lat_total) + first_row) / POLAR
+    colatitude = colatitude.reshape(lat_devices, rows).T.reshape(-1)
+    quad_weight = 2.0 * math.pi * math.pi / POLAR * np.sin(colatitude)
+    index = np.arange(1, M)
+    terms = np.concatenate([[0.0], np.log((2.0 * index + 1.0) / (2.0 * index))])
+    log_norm = -0.5 * math.log(4.0 * math.pi) + 0.5 * np.cumsum(terms)
+    orders = np.stack([owned_orders(a, per_device, lat_devices) for a in range(lat_devices)], axis=0)
+    start = np.exp(log_norm)[np.concatenate([orders, orders], axis=1)]
+    start = np.broadcast_to(start[:, :, None], start.shape + (lat_total,)).astype(np.float32)
+    rows_of = np.stack([np.cos(colatitude), np.log(np.sin(colatitude))], axis=0)
+    rows_of = np.broadcast_to(rows_of[:, None, :], (2, 8, lat_total)).astype(np.float32)
+    quad = np.broadcast_to(quad_weight[:, None], (lat_total, 128)).astype(np.float32)
+    return (start, rows_of, quad)
 
 
 def filter_coeff(filters, disco_weight, band_start, band_reach, first_row, lat_total):
@@ -64,17 +64,21 @@
     target = first_row + jnp.arange(count, dtype=jnp.int32)[:, None] + offsets[None, :]
     inside = (target >= 0) & (target < lat_total)
     chosen = jnp.where(live[:, :, None] & place & inside[:, None, :], 1.0, 0.0)
-    placed = jnp.einsum("ikrt,iro->ikot", filters, chosen, precision=highest)
-    placed = jnp.pad(placed, ((0, 0), (0, 0), (0, 0), (0, TAPS - KLON)))
-    return jnp.einsum("ikot,kc->iotc", placed, disco_weight, precision=highest)
+    total = jnp.zeros((count, SPAN, TAPS, disco_weight.shape[1]), f32)
+    taps = jnp.pad(filters, ((0, 0), (0, 0), (0, 0), (0, TAPS - KLON)))
+    for k in range(filters.shape[1]):
+        placed = jnp.zeros((count, SPAN, TAPS), f32)
+        for r in range(WIN):
+            placed = placed + chosen[:, r, :, None] * taps[:, k, r][:, None, :]
+        total = total + placed[..., None] * disco_weight[k]
+    return total
 
 
 def owned_orders(lat_index, per_device, devices):
     per_class = devices // 4
     kind = lat_index // per_class
-    kind_order = jnp.where(kind == 1, 2, jnp.where(kind == 2, 1, kind))
-    local = (lat_index % per_class) * per_device + jnp.arange(per_device, dtype=jnp.int32)
-    return kind_order + 4 * local
+    kind_order = (0, 2, 1, 3)[kind]
+    return kind_order + 4 * ((lat_index % per_class) * per_device + np.arange(per_device))
 
 
 def halves(array):
@@ -130,13 +134,14 @@
 
 
 def layer_kernel(
-    f_ref, cot_ref, w_ref, coef_ref, gain_ref, small_ref, qw_ref, tf_ref, ti_ref,
+    f_ref, cot_any, w_ref, coef_ref, gain_any, start_ref, rows_ref, quad_ref, tf_any, ti_any,
     out_ref, gin_ref, gw_ref,
     z1, g1, y1, h1, z2, g2, y2, h2,
     s1, r1, o1, c1, s2, r2, o2, c2,
     wsend, wrecv, wpart, wall, wmine,
     fext, eext, cext, local, gpad, ft_ref, leg_ref, l2_ref, lt_ref,
-    chan_send, chan_recv, lat_send, lat_recv, own_sem, halo_send, halo_recv, coef_send, coef_recv,
+    cot_ref, tf_ref, ti_ref, gain_all, gain_ref,
+    load_sem, chan_send, chan_recv, lat_send, lat_recv, own_sem, halo_send, halo_recv, coef_send, coef_recv,
 ):
     devices = lax.axis_size("lat")
     me = lax.axis_index("lat")
@@ -150,6 +155,12 @@
     right = lax.rem(mine + 1, 4)
     left = lax.rem(mine + 3, 4)
 
+    loads = []
+    for index, (source, target) in enumerate(
+        ((tf_any, tf_ref), (gain_any, gain_all), (ti_any, ti_ref), (cot_any, cot_ref))
+    ):
+        loads.append(pltpu.make_async_copy(source, target, load_sem.at[index]))
+
     barrier = pltpu.get_barrier_semaphore()
 
     def greet(k, carry):
@@ -166,6 +177,9 @@
     def pack(buffer, i, h, pair):
         buffer[2 * h, pl.ds(i, pair[0].shape[0]), :] = pair[0]
         buffer[2 * h + 1, pl.ds(i, pair[0].shape[0]), :] = pair[1]
+
+    for load in loads:
+        load.start()
 
     w_high, w_low = split(w_ref[...])
     mixed = []
@@ -230,6 +244,10 @@
     def lat_drain(stage, target, size):
         sent = target.at[pl.ds(0, size * (devices - 1))]
         pltpu.make_async_copy(sent, sent, lat_send.at[stage]).wait()
+
+    group = min(8, devices)
+    place = lax.rem(me, group)
+    far = (place == group - 1, place == 0)
 
     def halo_start(stage, ext, field):
         whole = pl.ds(EDGE, quarter)
@@ -253,9 +271,16 @@
                 recv_sem=halo_recv.at[stage, index],
                 device_id={"lat": a, "chan": b},
             )
-            copy.start()
+            if index < 6:
+                copy.start()
+            else:
+                pl.when(jnp.logical_not(far[index - 6]))(copy.start)
             copies.append(copy)
         return copies
+
+    def halo_far(copies):
+        pl.when(far[0])(copies[6].start)
+        pl.when(far[1])(copies[7].start)
 
     first_exchange = chan_start(0, z1, g1)
     own_field = pltpu.make_async_copy(f_ref, fext.at[pl.ds(2, 2), pl.ds(EDGE, quarter)], own_sem.at[4])
@@ -275,7 +300,14 @@
         coef_copies.append(copy)
     field_halo = halo_start(0, fext, lambda cols: f_ref.at[:, cols])
 
-    order, start, log_start, cosine = (small_ref[0], small_ref[1], small_ref[2], small_ref[3])
+    per_class = devices // 4
+    kind = me // per_class
+    kind_order = jnp.where(kind == 1, 2, jnp.where(kind == 2, 1, kind))
+    first_order = kind_order + 16 * lax.rem(me, per_class)
+    slot = lax.broadcasted_iota(jnp.int32, (8, leg_ref.shape[1]), 0)
+    order = (first_order + 4 * lax.rem(slot, 4)).astype(f32)
+    start, cosine = (start_ref[me], rows_ref[0])
+    log_start = order * rows_ref[1]
     order_square = order * order
     zeros = jnp.zeros_like(order)
 
@@ -305,7 +337,15 @@
         return (previous, second, log_scale)
 
     lax.fori_loop(0, L // STEPS, recur, (zeros, zeros, log_start))
-    lats = 2 * devices
+    loads[1].wait()
+    gain = gain_all[:, pl.ds(pl.multiple_of(128 * (mine // 2), 128), 128)]
+    low_half, high_half = swap_halves(gain, gain)
+    gain_ref[pl.ds(0, L), :] = jnp.where(lax.rem(mine, 2) == 0, low_half, high_half)
+    if lp > L:
+        gain_ref[pl.ds(L, lp - L), :] = jnp.zeros((lp - L, 128), f32)
+    order_weight = [
+        jnp.where(first_order + 4 * m == 0, 1.0, 2.0) / (4.0 * quarter) for m in range(4)
+    ]
     if lp > L:
         leg_ref[pl.ds(8 * L, 8 * (lp - L)), :] = jnp.zeros((8 * (lp - L), leg_ref.shape[1]), f32)
     for m in range(4):
@@ -369,22 +409,23 @@
             r_1 = spec[pl.ds(2 * m + 1, devices, stride=8), :]
             x = jnp.concatenate(swap_halves(r_0, r_1), axis=0)
             if weigh_first:
-                x = x * qw_ref[m]
+                x = x * (quad_ref[...] * order_weight[m])
             data = side_by_side(x)
             data = jnp.concatenate([data, data], axis=0)
             degree = folded(dot(l2_ref[m], data)) * gain_ref[...]
             data = side_by_side(degree)
             s = folded(dot(lt_ref[m, 0], data) + dot(lt_ref[m, 1], data))
             if not weigh_first:
-                s = s * qw_ref[m]
+                s = s * (quad_ref[...] * order_weight[m])
             t_0, t_1 = swap_halves(s[:devices], s[devices:])
             result[pl.ds(2 * m, devices, stride=8), :] = t_0
             result[pl.ds(2 * m + 1, devices, stride=8), :] = t_1
 
-    def spectral_path(exchange, stage, grid, spec, arrived, back, returned, result, final, weigh_first):
+    def spectral_path(exchange, stage, grid, spec, arrived, back, returned, result, final, weigh_first, halo):
         chan_wait(exchange)
         waves_forward(grid, spec)
         lat_start(stage, spec, arrived, 8)
+        halo_far(halo)
         lat_wait(stage, arrived)
         legendre_pair(arrived, back, weigh_first)
         lat_start(stage + 1, back, returned, 8)
@@ -408,7 +449,9 @@
                         totals[i] = term if totals[i] is None else totals[i] + term
         return totals
 
-    second_exchange = spectral_path(first_exchange, 0, g1, s1, r1, o1, c1, y1, h1, True)
+    loads[0].wait()
+    loads[2].wait()
+    second_exchange = spectral_path(first_exchange, 0, g1, s1, r1, o1, c1, y1, h1, True, field_halo)
 
     own_field.wait()
     for copy in field_halo:
@@ -425,6 +468,7 @@
     lax.fori_loop(0, quarter // step, forward_local, 0)
 
     chan_wait(second_exchange)
+    loads[3].wait()
 
     def pointwise(index, carry):
         n = pl.multiple_of(index * step, 8)
@@ -451,7 +495,7 @@
         return eext.at[pl.ds(2, 2), pl.ds(cols.start + EDGE, cols.size)]
 
     error_halo = halo_start(1, eext, error_part)
-    last_exchange = spectral_path(third_exchange, 2, g2, s2, r2, o2, c2, y2, h2, False)
+    last_exchange = spectral_path(third_exchange, 2, g2, s2, r2, o2, c2, y2, h2, False, error_halo)
 
     own_coef.wait()
     for copy in coef_copies + error_halo:
@@ -542,35 +586,11 @@
     chan_devices = lax.axis_size("chan")
     lat_total = rows * lat_devices
     lon_total = quarter * chan_devices
-    part = chans // chan_devices
     per_device = M // lat_devices
     qp, lp = (padded_size(quarter), padded_size(L))
     me = lax.axis_index("lat")
 
-    colatitude, quad_weight = grid_tables(lat_total)
-    colatitude = colatitude.reshape(lat_devices, rows).T.reshape(-1)
-    quad_weight = quad_weight.reshape(lat_devices, rows).T.reshape(-1)
-    orders = owned_orders(me, per_device, lat_devices)
-    one_hot = (orders[:, None] == jnp.arange(M, dtype=jnp.int32)[None, :]).astype(f32)
-    log_norm = jnp.sum(one_hot * log_norms(M)[None, :], axis=1)
-    order_f = orders.astype(f32)[:, None]
-    shape = (per_device, lat_total)
-    small = jnp.stack(
-        [
-            jnp.broadcast_to(order_f, shape),
-            jnp.broadcast_to(jnp.exp(log_norm)[:, None], shape),
-            order_f * jnp.log(jnp.sin(colatitude))[None, :],
-            jnp.broadcast_to(jnp.cos(colatitude)[None, :], shape),
-        ],
-        axis=0,
-    )
-    small = jnp.concatenate([small, small], axis=1)
-    order_weight = jnp.where(orders == 0, 1.0, 2.0).astype(f32) / lon_total
-    qw = jnp.broadcast_to(
-        order_weight[:, None, None] * quad_weight[None, :, None], (per_device, lat_total, 128)
-    )
-    gain = lax.dynamic_slice_in_dim(degree_gain, lax.axis_index("chan") * part, part, axis=1)
-    gain = jnp.pad(jnp.concatenate([gain, gain], axis=1), ((0, lp - L), (0, 0)))
+    start, rows_of, quad = geometry(lat_devices, rows, per_device)
     coefficient = filter_coeff(
         filters, disco_weight, band_start, band_reach, me * rows, lat_total
     )
@@ -600,6 +620,12 @@
             pltpu.VMEM((8 * lp, lat_total), f32),
             pltpu.VMEM((4, lp, 2 * lat_total), bf16),
             pltpu.VMEM((4, 2, lat_total, lp), bf16),
+            pltpu.VMEM((rows, quarter, chans), f32),
+            pltpu.VMEM(tables.shape, bf16),
+            pltpu.VMEM(inverse.shape, bf16),
+            pltpu.VMEM((L, chans), f32),
+            pltpu.VMEM((lp, 128), f32),
+            dma((4,)),
             dma((5, 4)),
             dma((5, 4)),
             dma((6,)),
@@ -612,6 +638,7 @@
         ]
     )
     vmem = pl.BlockSpec(memory_space=pltpu.VMEM)
+    hbm = pl.BlockSpec(memory_space=pl.ANY)
     return pl.pallas_call(
         layer_kernel,
         out_shape=(
@@ -619,7 +646,7 @@
             jax.ShapeDtypeStruct(grid_field.shape, f32),
             jax.ShapeDtypeStruct((chans, chans), f32),
         ),
-        in_specs=[vmem] * 9,
+        in_specs=[vmem, hbm, vmem, vmem, hbm, vmem, vmem, vmem, hbm, hbm],
         out_specs=(vmem, vmem, vmem),
         scratch_shapes=scratch,
         compiler_params=pltpu.CompilerParams(
@@ -631,9 +658,10 @@
         cotangent,
         spec_weight,
         coefficient,
-        gain,
-        small,
-        qw,
+        degree_gain,
+        jnp.asarray(start),
+        jnp.asarray(rows_of),
+        jnp.asarray(quad),
         jnp.asarray(tables),
         jnp.asarray(inverse),
     )

time: 168 us -> 164 us (0.976)
  matrix products: 2.6 us -> 0 us
    dot_general x2 -> x0, matrix products: 2.6 us -> none  [the longest x1 1.6 us: filter_coeff(): return jnp.einsum('ikot,kc->iotc', placed, disco_weight, precision=highest)]
    slice x1 -> x3, local copies, waits for them, and re-layouts: 0.07 us -> 2.42 us  [the longest x2 1.58 us: filter_coeff(): placed = placed + chosen[:, r, :, None] * taps[:, k, r][:, None, :]]
    unnamed x10 -> x7, local copies, waits for them, and re-layouts: 3.7 us -> 3.68 us
where the time goes in v1:
time: 164 us
  Pallas kernels  155 us (95%)
  local copies, waits for them, and re-layouts  6.11 us (4%)
  other arithmetic  2.31 us (1%)
    pallas_call x1, Pallas kernels, body(): pl.pallas_call(layer_kernel, out_shape=(jax.ShapeDtypeStruct(grid_field.s...  155 us
    unnamed x7, local copies, waits for them, and re-layouts  3.68 us

profile of v1, /device:TPU:1, one launch (start us, length us, event | category | flops | bytes accessed | tf_op | source)
XLA Modules:
  0.0 163.8 jit_solution(14134107427544393124)
XLA Ops:
  0.7 0.1 compare_and_fusion
  0.7 0.7 iota_compare_fusion
  1.4 0.7 iota_add_fusion
  2.1 0.1 and_select_fusion
  2.1 0.7 pad_slice_fusion.2
  2.9 0.8 fusion
  3.7 0.9 pad_slice_fusion.11
  4.6 0.1 multiply_add_fusion.4
  4.6 0.7 multiply_add_fusion.coef_ref
  5.4 154.7 %layer.1 = (f32[2,360,256]{2,1,0:T(8,128)}, f32[2,360,256]{2,1,0:T(8,128)}, f32[256,256]{1,0:T(8,128)}) custom-call(f32[2,360,256]{2,1,0:T(8,128)} %f_ref.1, f32[2,360,256]{2,1,0:T(8,128)} %cot_any.1, f32[256,256]{1,0:T(8,128)} %w_ref.1, f32[2,5,8,256]{3,2,1,0:T(8,128)} %multiply_add_fusion.coef_ref, f32[360,256]{1,0:T(8,128)} %gain_any.1, ...), custom_call_target="tpu_custom_call" | custom-call | tf_op jit(solution)/shard_map/layer/pallas_call | solution.py:642
  160.1 0.0 copy-start
  160.1 0.0 copy-start.1
  160.1 2.1 %copy.19 = f32[2,360,256]{2,1,0:T(8,128)} copy(f32[2,360,256]{2,1,0:T(8,128)} %get-tuple-element.29) | data formatting | bytes 1474560
  162.2 0.0 copy-done
  162.2 0.9 copy.20
  163.1 0.0 copy-done.1
  163.1 0.7 copy.21
  (3 shorter events, 0.0 us)
Async XLA Ops:
  160.1 2.1 %copy-start = (f32[2,360,256]{2,1,0:T(8,128)S(1)}, f32[2,360,256]{2,1,0:T(8,128)}, u32[]{:S(2)}) copy-start(f32[2,360,256]{2,1,0:T(8,128)} %get-tuple-element.30) | copy-start | bytes 2211844
  160.1 3.0 %copy-start.1 = (f32[256,256]{1,0:T(8,128)S(1)}, f32[256,256]{1,0:T(8,128)}, u32[]{:S(2)}) copy-start(f32[256,256]{1,0:T(8,128)} %get-tuple-element.31) | copy-start | bytes 786436

commit v2 on v1

--- a/solution.py
+++ b/solution.py
@@ -33,6 +33,10 @@
     return -(-n // 128) * 128
 
 
+def half_rows(n):
+    return -(-n // 16) * 8
+
+
 def chunk_rows(n):
     return 72 if n % 72 == 0 else n
 
@@ -48,30 +52,11 @@
     log_norm = -0.5 * math.log(4.0 * math.pi) + 0.5 * np.cumsum(terms)
     orders = np.stack([owned_orders(a, per_device, lat_devices) for a in range(lat_devices)], axis=0)
     start = np.exp(log_norm)[np.concatenate([orders, orders], axis=1)]
-    start = np.broadcast_to(start[:, :, None], start.shape + (lat_total,)).astype(np.float32)
+    start = np.ascontiguousarray(start.T).astype(np.float32)
     rows_of = np.stack([np.cos(colatitude), np.log(np.sin(colatitude))], axis=0)
     rows_of = np.broadcast_to(rows_of[:, None, :], (2, 8, lat_total)).astype(np.float32)
     quad = np.broadcast_to(quad_weight[:, None], (lat_total, 128)).astype(np.float32)
     return (start, rows_of, quad)
-
-
-def filter_coeff(filters, disco_weight, band_start, band_reach, first_row, lat_total):
-    count = filters.shape[0]
-    rows = jnp.arange(WIN, dtype=jnp.int32)
-    offsets = jnp.arange(SPAN, dtype=jnp.int32) - HMAX
-    live = rows[None, :] < band_reach[:, None]
-    place = (band_start[:, None] + rows[None, :])[:, :, None] == offsets[None, None, :]
-    target = first_row + jnp.arange(count, dtype=jnp.int32)[:, None] + offsets[None, :]
-    inside = (target >= 0) & (target < lat_total)
-    chosen = jnp.where(live[:, :, None] & place & inside[:, None, :], 1.0, 0.0)
-    total = jnp.zeros((count, SPAN, TAPS, disco_weight.shape[1]), f32)
-    taps = jnp.pad(filters, ((0, 0), (0, 0), (0, 0), (0, TAPS - KLON)))
-    for k in range(filters.shape[1]):
-        placed = jnp.zeros((count, SPAN, TAPS), f32)
-        for r in range(WIN):
-            placed = placed + chosen[:, r, :, None] * taps[:, k, r][:, None, :]
-        total = total + placed[..., None] * disco_weight[k]
-    return total
 
 
 def owned_orders(lat_index, per_device, devices):
@@ -103,7 +88,7 @@
             second.append(np.stack([-sign * sine, -sign * cosine], axis=1).reshape(M // 2, quarter))
     table = np.concatenate(plain + first + second, axis=0)
     table = np.pad(table, ((0, 0), (0, padded_size(quarter) - quarter)))
-    return (halves(table), halves(np.ascontiguousarray(table.T)))
+    return halves(table)
 
 
 def split(x):
@@ -121,33 +106,40 @@
     return jnp.dot(a, b, preferred_element_type=f32)
 
 
+def lane(x):
+    return lax.broadcasted_iota(jnp.int32, x.shape, 1)
+
+
+def both(x):
+    high = x.astype(bf16).astype(f32)
+    return jnp.where(lane(x) < 64, high, x - high).astype(bf16)
+
+
 def folded(y):
-    half = y.shape[1] // 2
-    return y[:, :half] + y[:, half:]
-
-
-def swap_halves(a, b):
-    low = lax.broadcasted_iota(jnp.int32, a.shape, 1) < 64
-    first = jnp.where(low, a, pltpu.roll(b, 64, 1))
-    second = jnp.where(low, pltpu.roll(a, 64, 1), b)
+    return y + pltpu.roll(y, 64, 1)
+
+
+def parted(a, b):
+    low = lax.rem(lane(a), 64) < 32
+    first = jnp.where(low, a, pltpu.roll(b, 32, 1))
+    second = jnp.where(low, pltpu.roll(a, 32, 1), b)
     return (first, second)
 
 
 def layer_kernel(
-    f_ref, cot_any, w_ref, coef_ref, gain_any, start_ref, rows_ref, quad_ref, tf_any, ti_any,
+    f_ref, cot_any, w_ref, filters_ref, disco_ref, start_row_ref, reach_ref, gain_any, start_ref, rows_ref, quad_ref, tf_any,
     out_ref, gin_ref, gw_ref,
-    z1, g1, y1, h1, z2, g2, y2, h2,
-    s1, r1, o1, c1, s2, r2, o2, c2,
+    blocks, lines,
     wsend, wrecv, wpart, wall, wmine,
     fext, eext, cext, local, gpad, ft_ref, leg_ref, l2_ref, lt_ref,
-    cot_ref, tf_ref, ti_ref, gain_all, gain_ref,
+    coef_ref, cot_ref, tf_ref, ti_ref, gain_all, gain_ref,
     load_sem, chan_send, chan_recv, lat_send, lat_recv, own_sem, halo_send, halo_recv, coef_send, coef_recv,
 ):
     devices = lax.axis_size("lat")
     me = lax.axis_index("lat")
     mine = lax.axis_index("chan")
     rows, quarter, chans = f_ref.shape
-    qp = g1.shape[1]
+    qp = gpad.shape[1]
     lp = l2_ref.shape[1]
     step = chunk_rows(quarter)
     up = lax.rem(me + 1, devices)
@@ -157,7 +149,7 @@
 
     loads = []
     for index, (source, target) in enumerate(
-        ((tf_any, tf_ref), (gain_any, gain_all), (ti_any, ti_ref), (cot_any, cot_ref))
+        ((tf_any, tf_ref), (gain_any, gain_all), (cot_any, cot_ref))
     ):
         loads.append(pltpu.make_async_copy(source, target, load_sem.at[index]))
 
@@ -174,22 +166,54 @@
         for b in (right, left):
             pl.semaphore_signal(barrier, inc=1, device_id={"lat": a, "chan": b})
 
-    def pack(buffer, i, h, pair):
-        buffer[2 * h, pl.ds(i, pair[0].shape[0]), :] = pair[0]
-        buffer[2 * h + 1, pl.ds(i, pair[0].shape[0]), :] = pair[1]
+    half_size = half_rows(quarter)
+    spare = 2 * half_size - quarter
+
+    def fold_rows(value):
+        second = value[half_size:]
+        if spare:
+            second = jnp.concatenate([second, jnp.zeros((spare, 64), f32)], axis=0)
+        return jnp.concatenate([value[:half_size], second], axis=1)
+
+    def open_rows(value):
+        left = lane(value) < 64
+        turned = pltpu.roll(value, 64, 1)
+        parts = [jnp.where(left, value, turned), jnp.where(left, turned, value)]
+        if qp > 2 * half_size:
+            parts.append(jnp.zeros((qp - 2 * half_size, 128), f32))
+        return jnp.concatenate(parts, axis=0)
+
+    def pack(buffer, pair):
+        for q in range(4):
+            lanes = slice(32 * q, 32 * q + 32)
+            buffer[q] = fold_rows(jnp.concatenate([pair[0][:, lanes], pair[1][:, lanes]], axis=1))
+
+    def unpack(buffer):
+        values = [buffer[q] for q in range(4)]
+        fields = []
+        for i in range(rows):
+            upper = [value[:, 32 * i : 32 * i + 32] for value in values]
+            lower = [value[: quarter - half_size, 64 + 32 * i : 96 + 32 * i] for value in values]
+            halves_of = [jnp.concatenate(upper, axis=1), jnp.concatenate(lower, axis=1)]
+            fields.append(jnp.concatenate(halves_of, axis=0))
+        return fields
+
+    w_high, w_low = split(w_ref[...])
+    fields = [split(f_ref[i]) for i in range(rows)]
+
+    def mix(s):
+        lanes = slice(128 * s, 128 * s + 128)
+        pair = []
+        for high, low in fields:
+            pair.append(
+                dot(high, w_high[:, lanes])
+                + (dot(low, w_high[:, lanes]) + dot(high, w_low[:, lanes]))
+            )
+        pack(blocks.at[0, s], pair)
 
     for load in loads:
         load.start()
-
-    w_high, w_low = split(w_ref[...])
-    mixed = []
-    for i in range(rows):
-        high, low = split(f_ref[i])
-        mixed.append(dot(high, w_high) + (dot(low, w_high) + dot(high, w_low)))
-    for h in range(2):
-        lanes = slice(128 * h, 128 * h + 128)
-        pack(z1, 0, h, swap_halves(mixed[0][:, lanes], mixed[1][:, lanes]))
-
+    mix(0)
     pl.semaphore_wait(barrier, devices - 1 + 3 + 4)
 
     def chan_start(stage, source, target):
@@ -197,8 +221,8 @@
         for k in (2, 1, 3):
             peer = lax.rem(mine + k, 4)
             copy = pltpu.make_async_remote_copy(
-                src_ref=source.at[peer, pl.ds(0, quarter)],
-                dst_ref=target.at[mine, pl.ds(0, quarter)],
+                src_ref=source.at[peer],
+                dst_ref=target.at[mine],
                 send_sem=chan_send.at[stage, k],
                 recv_sem=chan_recv.at[stage, k],
                 device_id={"chan": peer},
@@ -206,7 +230,7 @@
             copy.start()
             copies.append(copy)
         own = pltpu.make_async_copy(
-            source.at[mine, pl.ds(0, quarter)], target.at[mine, pl.ds(0, quarter)], own_sem.at[stage]
+            source.at[mine], target.at[mine], own_sem.at[stage]
         )
         own.start()
         return (copies, own)
@@ -282,10 +306,32 @@
         pl.when(far[0])(copies[6].start)
         pl.when(far[1])(copies[7].start)
 
-    first_exchange = chan_start(0, z1, g1)
-    own_field = pltpu.make_async_copy(f_ref, fext.at[pl.ds(2, 2), pl.ds(EDGE, quarter)], own_sem.at[4])
+    first_exchange = chan_start(0, blocks.at[0, 0], blocks.at[1, 0])
+    mix(1)
+    own_field = pltpu.make_async_copy(f_ref, fext.at[pl.ds(2, 2), pl.ds(EDGE, quarter)], own_sem.at[8])
     own_field.start()
-    own_coef = pltpu.make_async_copy(coef_ref, cext.at[pl.ds(2, 2)], own_sem.at[5])
+    disco = [disco_ref[pl.ds(k, 1), :] for k in range(disco_ref.shape[0])]
+    for i in range(rows):
+        chosen = {}
+        for o in range(SPAN):
+            target = me * rows + i + o - HMAX
+            inside = jnp.where(target >= 0, 1.0, 0.0) * jnp.where(target < rows * devices, 1.0, 0.0)
+            for r in range(WIN):
+                live = jnp.where(r < reach_ref[i], inside, 0.0)
+                chosen[o, r] = jnp.where(start_row_ref[i] + r == o - HMAX, live, 0.0)
+        for o in range(SPAN):
+            taps = []
+            for t in range(KLON):
+                line = None
+                for k in range(len(disco)):
+                    factor = filters_ref[i, k, 0, t] * chosen[o, 0]
+                    for r in range(1, WIN):
+                        factor = factor + filters_ref[i, k, r, t] * chosen[o, r]
+                    line = factor * disco[k] if line is None else line + factor * disco[k]
+                taps.append(line)
+            taps.append(jnp.zeros((TAPS - KLON, chans), f32))
+            coef_ref[i, o] = jnp.concatenate(taps, axis=0)
+    own_coef = pltpu.make_async_copy(coef_ref, cext.at[pl.ds(2, 2)], own_sem.at[9])
     own_coef.start()
     coef_copies = []
     for index, (peer, row) in enumerate(((up, 0), (down, 4))):
@@ -306,7 +352,9 @@
     first_order = kind_order + 16 * lax.rem(me, per_class)
     slot = lax.broadcasted_iota(jnp.int32, (8, leg_ref.shape[1]), 0)
     order = (first_order + 4 * lax.rem(slot, 4)).astype(f32)
-    start, cosine = (start_ref[me], rows_ref[0])
+    device = lax.broadcasted_iota(jnp.int32, start_ref.shape, 1)
+    start = jnp.sum(jnp.where(device == me, start_ref[...], 0.0), axis=1, keepdims=True)
+    start, cosine = (start + jnp.zeros_like(order), rows_ref[0])
     log_start = order * rows_ref[1]
     order_square = order * order
     zeros = jnp.zeros_like(order)
@@ -338,11 +386,14 @@
 
     lax.fori_loop(0, L // STEPS, recur, (zeros, zeros, log_start))
     loads[1].wait()
-    gain = gain_all[:, pl.ds(pl.multiple_of(128 * (mine // 2), 128), 128)]
-    low_half, high_half = swap_halves(gain, gain)
-    gain_ref[pl.ds(0, L), :] = jnp.where(lax.rem(mine, 2) == 0, low_half, high_half)
-    if lp > L:
-        gain_ref[pl.ds(L, lp - L), :] = jnp.zeros((lp - L, 128), f32)
+    for s in range(2):
+        gain = gain_all[:, pl.ds(128 * s, 128)]
+        chosen = gain[:, 96:]
+        for q in range(3):
+            chosen = jnp.where(mine == q, gain[:, 32 * q : 32 * q + 32], chosen)
+        gain_ref[s, pl.ds(0, L), :] = jnp.concatenate([chosen] * 4, axis=1)
+        if lp > L:
+            gain_ref[s, pl.ds(L, lp - L), :] = jnp.zeros((lp - L, 128), f32)
     order_weight = [
         jnp.where(first_order + 4 * m == 0, 1.0, 2.0) / (4.0 * quarter) for m in range(4)
     ]
@@ -358,19 +409,13 @@
         field = f_ref[i]
         if qp > quarter:
             field = jnp.concatenate([field, jnp.zeros((qp - quarter, chans), f32)], axis=0)
-            gpad[i, pl.ds(quarter, qp - quarter), :] = jnp.zeros((qp - quarter, chans), f32)
+            gpad[i, pl.ds(quarter, qp - quarter), :] = jnp.zeros((qp - quarter, 128), f32)
         high, low = split(field.T)
         ft_ref[i, 0] = high
         ft_ref[i, 1] = low
 
     def waves_forward(grid, spec):
-        def block(q):
-            value = grid[q, pl.ds(0, quarter), :]
-            if qp > quarter:
-                value = jnp.concatenate([value, jnp.zeros((qp - quarter, 128), f32)], axis=0)
-            return value
-
-        g_0, g_1, g_2, g_3 = (block(0), block(1), block(2), block(3))
+        g_0, g_1, g_2, g_3 = [open_rows(grid[q]) for q in range(4)]
         even, odd = (g_0 + g_2, g_1 + g_3)
         half = 2 * devices
 
@@ -378,9 +423,9 @@
             band = pl.ds(first, count)
             return dot(tf_ref[0, band, :], data) + dot(tf_ref[1, band, :], data)
 
-        spec[pl.ds(0, half), :] = folded(apply(0, half, side_by_side(even + odd)))
-        spec[pl.ds(half, half), :] = folded(apply(half, half, side_by_side(even - odd)))
-        u, v = (side_by_side(g_0 - g_2), side_by_side(g_1 - g_3))
+        spec[pl.ds(0, half), :] = folded(apply(0, half, both(even + odd)))
+        spec[pl.ds(half, half), :] = folded(apply(half, half, both(even - odd)))
+        u, v = (both(g_0 - g_2), both(g_1 - g_3))
         spec[pl.ds(2 * half, 2 * half), :] = folded(
             apply(2 * half, 2 * half, u) + apply(4 * half, 2 * half, v)
         )
@@ -394,44 +439,57 @@
                 + dot(ti_ref[1, :, first : first + count], data)
             )
 
-        plain = apply(0, half, side_by_side(spec[pl.ds(0, half), :]))
-        other = apply(half, half, side_by_side(spec[pl.ds(half, half), :]))
-        cross = side_by_side(spec[pl.ds(2 * half, 2 * half), :])
+        plain = apply(0, half, both(spec[pl.ds(0, half), :]))
+        other = apply(half, half, both(spec[pl.ds(half, half), :]))
+        cross = both(spec[pl.ds(2 * half, 2 * half), :])
         u = apply(2 * half, 2 * half, cross)
         v = apply(4 * half, 2 * half, cross)
         even, odd = (plain + other, plain - other)
         for q, value in enumerate((even + u, odd + v, even - u, odd - v)):
-            grid[q] = value
-
-    def legendre_pair(spec, result, weigh_first):
+            upper, lower = (value[:half_size], value[half_size : 2 * half_size])
+            grid[q] = jnp.where(lane(upper) < 64, upper, lower)
+
+    def legendre_pair(spec, result, s, weigh_first):
         for m in range(4):
             r_0 = spec[pl.ds(2 * m, devices, stride=8), :]
             r_1 = spec[pl.ds(2 * m + 1, devices, stride=8), :]
-            x = jnp.concatenate(swap_halves(r_0, r_1), axis=0)
+            x = jnp.concatenate(parted(r_0, r_1), axis=0)
             if weigh_first:
                 x = x * (quad_ref[...] * order_weight[m])
-            data = side_by_side(x)
+            data = both(x)
             data = jnp.concatenate([data, data], axis=0)
-            degree = folded(dot(l2_ref[m], data)) * gain_ref[...]
-            data = side_by_side(degree)
-            s = folded(dot(lt_ref[m, 0], data) + dot(lt_ref[m, 1], data))
+            degree = folded(dot(l2_ref[m], data)) * gain_ref[s]
+            data = both(degree)
+            profile = folded(dot(lt_ref[m, 0], data) + dot(lt_ref[m, 1], data))
             if not weigh_first:
-                s = s * (quad_ref[...] * order_weight[m])
-            t_0, t_1 = swap_halves(s[:devices], s[devices:])
+                profile = profile * (quad_ref[...] * order_weight[m])
+            t_0, t_1 = parted(profile[:devices], profile[devices:])
             result[pl.ds(2 * m, devices, stride=8), :] = t_0
             result[pl.ds(2 * m + 1, devices, stride=8), :] = t_1
 
-    def spectral_path(exchange, stage, grid, spec, arrived, back, returned, result, final, weigh_first, halo):
-        chan_wait(exchange)
-        waves_forward(grid, spec)
-        lat_start(stage, spec, arrived, 8)
+    def spectral_path(first, way, halo):
+        base = 4 * way
+        chan_wait(first)
+        waves_forward(blocks.at[base + 1, 0], lines.at[base, 0])
+        lat_start(base, lines.at[base, 0], lines.at[base + 1, 0], 8)
+        second = chan_start(2 * way + 4, blocks.at[base, 1], blocks.at[base + 1, 1])
+        lat_wait(base, lines.at[base + 1, 0])
+        legendre_pair(lines.at[base + 1, 0], lines.at[base + 2, 0], 0, way == 0)
+        lat_start(base + 1, lines.at[base + 2, 0], lines.at[base + 3, 0], 8)
+        chan_wait(second)
+        waves_forward(blocks.at[base + 1, 1], lines.at[base, 1])
+        lat_start(base + 2, lines.at[base, 1], lines.at[base + 1, 1], 8)
         halo_far(halo)
-        lat_wait(stage, arrived)
-        legendre_pair(arrived, back, weigh_first)
-        lat_start(stage + 1, back, returned, 8)
-        lat_wait(stage + 1, returned)
-        waves_inverse(returned, result)
-        return chan_start(stage + 1, result, final)
+        lat_wait(base + 1, lines.at[base + 3, 0])
+        waves_inverse(lines.at[base + 3, 0], blocks.at[base + 2, 0])
+        lat_wait(base + 2, lines.at[base + 1, 1])
+        legendre_pair(lines.at[base + 1, 1], lines.at[base + 2, 1], 1, way == 0)
+        lat_start(base + 3, lines.at[base + 2, 1], lines.at[base + 3, 1], 8)
+        outgoing = [chan_start(2 * way + 1, blocks.at[base + 2, 0], blocks.at[base + 3, 0])]
+        lat_wait(base + 3, lines.at[base + 3, 1])
+        waves_inverse(lines.at[base + 3, 1], blocks.at[base + 2, 1])
+        outgoing.append(chan_start(2 * way + 5, blocks.at[base + 2, 1], blocks.at[base + 3, 1]))
+        return ([first, second], outgoing)
 
     def local_filter(ext, weights, adjoint, n, h):
         lanes = pl.ds(128 * h, 128)
@@ -450,8 +508,12 @@
         return totals
 
     loads[0].wait()
-    loads[2].wait()
-    second_exchange = spectral_path(first_exchange, 0, g1, s1, r1, o1, c1, y1, h1, True, field_halo)
+    width = min(128, 2 * devices)
+    for k in range(2):
+        for first in range(0, tf_ref.shape[1], width):
+            part = tf_ref[k, pl.ds(first, width), :].astype(f32)
+            ti_ref[k, :, pl.ds(first, width)] = part.T.astype(bf16)
+    exchanges = list(spectral_path(first_exchange, 0, field_halo))
 
     own_field.wait()
     for copy in field_halo:
@@ -467,35 +529,38 @@
 
     lax.fori_loop(0, quarter // step, forward_local, 0)
 
-    chan_wait(second_exchange)
-    loads[3].wait()
-
-    def pointwise(index, carry):
-        n = pl.multiple_of(index * step, 8)
-        band = pl.ds(n, step)
-        for h in range(2):
-            lanes = pl.ds(128 * h, 128)
-            spectral = swap_halves(h1[2 * h, band, :], h1[2 * h + 1, band, :])
-            errors = []
+    loads[2].wait()
+
+    def pointwise(s):
+        lanes = pl.ds(128 * s, 128)
+        for i, value in enumerate(unpack(blocks.at[3, s])):
+            local[i, :, lanes] = local[i, :, lanes] + value
+
+        def some_rows(index, carry):
+            n = pl.multiple_of(index * step, 8)
+            band = pl.ds(n, step)
             for i in range(rows):
-                hidden = local[i, band, lanes] + spectral[i]
+                hidden = local[i, band, lanes]
                 gate = 1.0 / (1.0 + jnp.exp(-hidden))
                 out_ref[i, band, lanes] = f_ref[i, band, lanes] + hidden * gate
                 error = cot_ref[i, band, lanes] * (gate * (1.0 + hidden * (1.0 - gate)))
                 eext[2 + i, pl.ds(pl.multiple_of(n + EDGE, 8), step), lanes] = error
-                errors.append(error)
-            pack(z2, n, h, swap_halves(errors[0], errors[1]))
-        return carry
-
-    lax.fori_loop(0, quarter // step, pointwise, 0)
-
-    third_exchange = chan_start(2, z2, g2)
+            return carry
+
+        lax.fori_loop(0, quarter // step, some_rows, 0)
+        pack(blocks.at[4, s], [eext[2 + i, pl.ds(EDGE, quarter), lanes] for i in range(rows)])
+
+    chan_wait(exchanges[1][0])
+    pointwise(0)
+    third_exchange = chan_start(2, blocks.at[4, 0], blocks.at[5, 0])
+    chan_wait(exchanges[1][1])
+    pointwise(1)
 
     def error_part(cols):
         return eext.at[pl.ds(2, 2), pl.ds(cols.start + EDGE, cols.size)]
 
     error_halo = halo_start(1, eext, error_part)
-    last_exchange = spectral_path(third_exchange, 2, g2, s2, r2, o2, c2, y2, h2, False, error_halo)
+    exchanges.extend(spectral_path(third_exchange, 1, error_halo))
 
     own_coef.wait()
     for copy in coef_copies + error_halo:
@@ -511,33 +576,35 @@
 
     lax.fori_loop(0, quarter // step, backward_local, 0)
 
-    chan_wait(last_exchange)
-    for h in range(2):
-        band = pl.ds(0, quarter)
-        pair = swap_halves(h2[2 * h, band, :], h2[2 * h + 1, band, :])
-        for i in range(rows):
-            gpad[i, band, pl.ds(128 * h, 128)] = pair[i]
-
-    weight = jnp.zeros((chans, chans), f32)
-    for i in range(rows):
-        high, low = split(gpad[i])
-        weight = weight + dot(ft_ref[i, 0], high) + (dot(ft_ref[i, 1], high) + dot(ft_ref[i, 0], low))
-    wsend[pl.ds(0, chans), :] = weight[:, :128]
-    wsend[pl.ds(chans, chans), :] = weight[:, 128:]
-    piece = 2 * chans // devices
-    lat_start(4, wsend, wrecv, piece)
-
     transposed = (((1,), (1,)), ((), ()))
 
     def dot_t(a, b):
         return lax.dot_general(a, b, transposed, preferred_element_type=f32)
 
-    for i in range(rows):
-        high, low = split(gpad[i, pl.ds(0, quarter), :])
-        grad = dot_t(high, w_high) + (dot_t(low, w_high) + dot_t(high, w_low))
-        gin_ref[i] = cot_ref[i] + local[i] + grad
-
-    lat_wait(4, wrecv)
+    piece = 2 * chans // devices
+    for s in range(2):
+        chan_wait(exchanges[3][s])
+        lanes = slice(128 * s, 128 * s + 128)
+        weight = jnp.zeros((chans, 128), f32)
+        grads = []
+        for i, value in enumerate(unpack(blocks.at[7, s])):
+            gpad[i, pl.ds(0, quarter), :] = value
+            high, low = split(gpad[i])
+            weight = weight + dot(ft_ref[i, 0], high) + (dot(ft_ref[i, 1], high) + dot(ft_ref[i, 0], low))
+            grads.append((high[:quarter], low[:quarter]))
+        wsend[pl.ds(s * chans, chans), :] = weight
+        if s == 1:
+            lat_start(8, wsend, wrecv, piece)
+        for i, (high, low) in enumerate(grads):
+            grad = dot_t(high, w_high[:, lanes]) + (
+                dot_t(low, w_high[:, lanes]) + dot_t(high, w_low[:, lanes])
+            )
+            if s == 0:
+                gin_ref[i] = cot_ref[i] + local[i] + grad
+            else:
+                gin_ref[i] = gin_ref[i] + grad
+
+    lat_wait(8, wrecv)
     total = wrecv[pl.ds(0, piece), :]
     for k in range(1, devices):
         total = total + wrecv[pl.ds(k * piece, piece), :]
@@ -548,13 +615,13 @@
         copy = pltpu.make_async_remote_copy(
             src_ref=wmine,
             dst_ref=wpart.at[mine],
-            send_sem=chan_send.at[4, k],
-            recv_sem=chan_recv.at[4, k],
+            send_sem=chan_send.at[8, k],
+            recv_sem=chan_recv.at[8, k],
             device_id={"chan": peer},
         )
         copy.start()
         copies.append(copy)
-    own = pltpu.make_async_copy(wmine, wpart.at[mine], own_sem.at[6])
+    own = pltpu.make_async_copy(wmine, wpart.at[mine], own_sem.at[10])
     own.start()
     own.wait()
     for copy in copies:
@@ -562,20 +629,23 @@
         copy.wait_send()
     wsum = wpart[0] + wpart[1] + wpart[2] + wpart[3]
     wmine[...] = wsum
-    lat_start(5, wmine, wall, piece, spread=True)
-    lat_wait(5, wall)
+    lat_start(9, wmine, wall, piece, spread=True)
+    lat_wait(9, wall)
     gw_ref[:, pl.ds(0, 128)] = wall[pl.ds(0, chans), :]
     gw_ref[:, pl.ds(128, 128)] = wall[pl.ds(chans, chans), :]
 
-    for handle in (first_exchange, second_exchange, third_exchange, last_exchange):
-        for copy in handle[0]:
-            copy.wait_send()
+    for handles in exchanges:
+        for handle in handles:
+            for copy in handle[0]:
+                copy.wait_send()
     for copy in field_halo + error_halo + coef_copies:
         copy.wait_send()
-    for stage, buffer in enumerate((s1, o1, s2, o2)):
-        lat_drain(stage, buffer, 8)
-    lat_drain(4, wsend, piece)
-    lat_drain(5, wall, piece)
+    for way in range(2):
+        for s in range(2):
+            lat_drain(4 * way + 2 * s, lines.at[4 * way, s], 8)
+            lat_drain(4 * way + 2 * s + 1, lines.at[4 * way + 2, s], 8)
+    lat_drain(8, wsend, piece)
+    lat_drain(9, wall, piece)
 
 
 def body(
@@ -588,23 +658,19 @@
     lon_total = quarter * chan_devices
     per_device = M // lat_devices
     qp, lp = (padded_size(quarter), padded_size(L))
-    me = lax.axis_index("lat")
 
     start, rows_of, quad = geometry(lat_devices, rows, per_device)
-    coefficient = filter_coeff(
-        filters, disco_weight, band_start, band_reach, me * rows, lat_total
-    )
-    tables, inverse = wave_tables(quarter, lon_total)
-
-    block = pltpu.VMEM((chan_devices, qp, 128), f32)
-    line = pltpu.VMEM((8 * lat_devices, 128), f32)
+    tables = wave_tables(quarter, lon_total)
+
     weights = pltpu.VMEM((2 * chans, 128), f32)
     piece = 2 * chans // lat_devices
     extended = pltpu.VMEM((rows + 2 * HMAX, quarter + 2 * EDGE, chans), f32)
     dma = pltpu.SemaphoreType.DMA
     scratch = (
-        [block] * 8
-        + [line] * 8
+        [
+            pltpu.VMEM((8, 2, chan_devices, half_rows(quarter), 128), f32),
+            pltpu.VMEM((8, 2, 8 * lat_devices, 128), f32),
+        ]
         + [
             weights,
             weights,
@@ -615,22 +681,23 @@
             extended,
             pltpu.VMEM((rows + 2 * HMAX, SPAN, TAPS, chans), f32),
             pltpu.VMEM((rows, quarter, chans), f32),
-            pltpu.VMEM((rows, qp, chans), f32),
+            pltpu.VMEM((rows, qp, 128), f32),
             pltpu.VMEM((rows, 2, chans, qp), bf16),
             pltpu.VMEM((8 * lp, lat_total), f32),
             pltpu.VMEM((4, lp, 2 * lat_total), bf16),
             pltpu.VMEM((4, 2, lat_total, lp), bf16),
+            pltpu.VMEM((rows, SPAN, TAPS, chans), f32),
             pltpu.VMEM((rows, quarter, chans), f32),
             pltpu.VMEM(tables.shape, bf16),
-            pltpu.VMEM(inverse.shape, bf16),
+            pltpu.VMEM((2, tables.shape[2], tables.shape[1]), bf16),
             pltpu.VMEM((L, chans), f32),
-            pltpu.VMEM((lp, 128), f32),
-            dma((4,)),
-            dma((5, 4)),
-            dma((5, 4)),
-            dma((6,)),
-            dma((6,)),
-            dma((7,)),
+            pltpu.VMEM((2, lp, 128), f32),
+            dma((3,)),
+            dma((9, 4)),
+            dma((9, 4)),
+            dma((10,)),
+            dma((10,)),
+            dma((11,)),
             dma((2, 8)),
             dma((2, 8)),
             dma((2,)),
@@ -638,6 +705,7 @@
         ]
     )
     vmem = pl.BlockSpec(memory_space=pltpu.VMEM)
+    smem = pl.BlockSpec(memory_space=pltpu.SMEM)
     hbm = pl.BlockSpec(memory_space=pl.ANY)
     return pl.pallas_call(
         layer_kernel,
@@ -646,7 +714,7 @@
             jax.ShapeDtypeStruct(grid_field.shape, f32),
             jax.ShapeDtypeStruct((chans, chans), f32),
         ),
-        in_specs=[vmem, hbm, vmem, vmem, hbm, vmem, vmem, vmem, hbm, hbm],
+        in_specs=[vmem, hbm, vmem, smem, vmem, smem, smem, hbm, vmem, vmem, vmem, hbm],
         out_specs=(vmem, vmem, vmem),
         scratch_shapes=scratch,
         compiler_params=pltpu.CompilerParams(
@@ -657,13 +725,15 @@
         grid_field,
         cotangent,
         spec_weight,
-        coefficient,
+        filters,
+        disco_weight,
+        band_start,
+        band_reach,
         degree_gain,
         jnp.asarray(start),
         jnp.asarray(rows_of),
         jnp.asarray(quad),
         jnp.asarray(tables),
-        jnp.asarray(inverse),
     )
 
 

time: 164 us -> 162 us (0.988)
  other arithmetic: 2.31 us -> 0 us
    slice x3 -> x0, local copies, waits for them, and re-layouts: 2.42 us -> none  [the longest x2 1.58 us: filter_coeff(): placed = placed + chosen[:, r, :, None] * taps[:, k, r][:, None, :]]
    unnamed x7 -> x8, local copies, waits for them, and re-layouts: 3.68 us -> 5 us
where the time goes in v2:
time: 162 us
  Pallas kernels  156 us (96%)
  local copies, waits for them, and re-layouts  5 us (3%)
    pallas_call x1, Pallas kernels, body(): pl.pallas_call(layer_kernel, out_shape=(jax.ShapeDtypeStruct(grid_field.s...  156 us
    unnamed x8, local copies, waits for them, and re-layouts  5 us

profile of v2, /device:TPU:1, one launch (start us, length us, event | category | flops | bytes accessed | tf_op | source)
XLA Modules:
  0.0 161.6 jit_solution(8354059446201912758)
XLA Ops:
  0.6 1.3 copy.15.filters_ref
  2.0 155.9 %layer.1 = (f32[2,360,256]{2,1,0:T(8,128)}, f32[2,360,256]{2,1,0:T(8,128)}, f32[256,256]{1,0:T(8,128)}) custom-call(f32[2,360,256]{2,1,0:T(8,128)} %f_ref.1, f32[2,360,256]{2,1,0:T(8,128)} %cot_any.1, f32[256,256]{1,0:T(8,128)} %w_ref.1, f32[2,4,3,5]{3,2,1,0:T(4,128)} %copy.15.filters_ref, f32[4,256]{1,0:T(4,128)} %disco_ref.1, s32[2]{0:T(128)} %start_row_ref.1, ...), custom_call_target="tpu_custom_call" | custom-call | tf_op jit(solution)/shard_map/layer/pallas_call | solution.py:710
  157.9 0.0 copy-start
  157.9 0.0 copy-start.1
  157.9 2.1 %copy.19 = f32[2,360,256]{2,1,0:T(8,128)} copy(f32[2,360,256]{2,1,0:T(8,128)} %get-tuple-element.6) | data formatting | bytes 1474560
  160.0 0.0 copy-done
  160.0 0.9 copy.20
  160.9 0.0 copy-done.1
  160.9 0.7 copy.21
Async XLA Ops:
  157.9 2.1 %copy-start = (f32[2,360,256]{2,1,0:T(8,128)S(1)}, f32[2,360,256]{2,1,0:T(8,128)}, u32[]{:S(2)}) copy-start(f32[2,360,256]{2,1,0:T(8,128)} %get-tuple-element.7) | copy-start | bytes 2211844
  157.9 3.0 %copy-start.1 = (f32[256,256]{1,0:T(8,128)S(1)}, f32[256,256]{1,0:T(8,128)}, u32[]{:S(2)}) copy-start(f32[256,256]{1,0:T(8,128)} %get-tuple-element.8) | copy-start | bytes 786436

commit v3 on v2

--- a/solution.py
+++ b/solution.py
@@ -261,6 +261,33 @@
             target.at[pl.ds(pl.multiple_of(me * size, 8), size)],
             lat_recv.at[stage],
         ).start()
+
+    def weight_start(h):
+        count = devices // 2
+        size = 2 * chans // devices
+
+        def send(k, carry):
+            peer = h * count + lax.rem(me + k, count)
+            source = wsend.at[pl.ds(pl.multiple_of(peer * size, 8), size)]
+            target = wrecv.at[pl.ds(pl.multiple_of(me * size, 8), size)]
+
+            @pl.when(peer != me)
+            def _():
+                pltpu.make_async_remote_copy(
+                    src_ref=source,
+                    dst_ref=target,
+                    send_sem=lat_send.at[8],
+                    recv_sem=lat_recv.at[8],
+                    device_id={"lat": peer},
+                ).start()
+
+            @pl.when(peer == me)
+            def _():
+                pltpu.make_async_copy(source, target, lat_recv.at[8]).start()
+
+            return carry
+
+        lax.fori_loop(0, count, send, 0)
 
     def lat_wait(stage, target):
         pltpu.make_async_copy(target, target, lat_recv.at[stage]).wait()
@@ -593,8 +620,7 @@
             weight = weight + dot(ft_ref[i, 0], high) + (dot(ft_ref[i, 1], high) + dot(ft_ref[i, 0], low))
             grads.append((high[:quarter], low[:quarter]))
         wsend[pl.ds(s * chans, chans), :] = weight
-        if s == 1:
-            lat_start(8, wsend, wrecv, piece)
+        weight_start(s)
         for i, (high, low) in enumerate(grads):
             grad = dot_t(high, w_high[:, lanes]) + (
                 dot_t(low, w_high[:, lanes]) + dot_t(high, w_low[:, lanes])

time: 162 us -> 162 us (level)
  no operation moved by 1% of the time
where the time goes in v3:
time: 162 us; the launch traced here: 161 us
  Pallas kernels  156 us (96%)
  local copies, waits for them, and re-layouts  5 us (3%)
    pallas_call x1, Pallas kernels, body(): pl.pallas_call(layer_kernel, out_shape=(jax.ShapeDtypeStruct(grid_field.s...  156 us
    unnamed x8, local copies, waits for them, and re-layouts  5 us

profile of v3, /device:TPU:1, one launch (start us, length us, event | category | flops | bytes accessed | tf_op | source)
XLA Modules:
  0.0 161.4 jit_solution(16008440876341802304)
XLA Ops:
  0.6 1.3 copy.15.filters_ref
  2.0 155.8 %layer.1 = (f32[2,360,256]{2,1,0:T(8,128)}, f32[2,360,256]{2,1,0:T(8,128)}, f32[256,256]{1,0:T(8,128)}) custom-call(f32[2,360,256]{2,1,0:T(8,128)} %f_ref.1, f32[2,360,256]{2,1,0:T(8,128)} %cot_any.1, f32[256,256]{1,0:T(8,128)} %w_ref.1, f32[2,4,3,5]{3,2,1,0:T(4,128)} %copy.15.filters_ref, f32[4,256]{1,0:T(4,128)} %disco_ref.1, s32[2]{0:T(128)} %start_row_ref.1, ...), custom_call_target="tpu_custom_call" | custom-call | tf_op jit(solution)/shard_map/layer/pallas_call | solution.py:736
  157.7 0.0 copy-start
  157.7 0.0 copy-start.1
  157.7 2.1 %copy.19 = f32[2,360,256]{2,1,0:T(8,128)} copy(f32[2,360,256]{2,1,0:T(8,128)} %get-tuple-element.6) | data formatting | bytes 1474560
  159.8 0.0 copy-done
  159.8 0.9 copy.20
  160.7 0.0 copy-done.1
  160.7 0.7 copy.21
Async XLA Ops:
  157.7 2.1 %copy-start = (f32[2,360,256]{2,1,0:T(8,128)S(1)}, f32[2,360,256]{2,1,0:T(8,128)}, u32[]{:S(2)}) copy-start(f32[2,360,256]{2,1,0:T(8,128)} %get-tuple-element.7) | copy-start | bytes 2211844
  157.7 3.0 %copy-start.1 = (f32[256,256]{1,0:T(8,128)S(1)}, f32[256,256]{1,0:T(8,128)}, u32[]{:S(2)}) copy-start(f32[256,256]{1,0:T(8,128)} %get-tuple-element.8) | copy-start | bytes 786436
